TPU v7x, 32 devices: a whole 2x2x4 slice. The times are simulated.
32 devices in a mesh: tile: 16 (over z, x, core), case: 2 (over y).
Axes of the slice: x: 2, y: 2, z: 4, core: 2. Of those that a mesh axis runs over, the one named last changes fastest.
Arguments:
- load: float32 [4, 3, 24576], P('case', None, 'tile')
- target: float32 [4, 3, 24576], P('case', None, 'tile'), may hold values from -6 to 6
- lame_lambda: float32 [24576], P('tile'), may hold values from 0.5 to 2
- lame_mu: float32 [24576], P('tile'), may hold values from 0.5 to 2
- volume: float32 [24576], P('tile'), may hold values from 0.5 to 2
- smooth: float32 [192, 4, 3, 128, 128], P('tile'), may hold values from -0.25 to 0.25
- columns: int32 [192, 4], P('tile'), may hold values from 0 to 27, as said below
- send_list: int32 [16, 2, 8], P('tile'), may hold values from 0 to 11, as said below
- counts: int32 [16], P('tile'), may hold values from 192 to 1536, as said below
Outputs:
- displacement: float32 [4, 3, 24576], P('case', None, 'tile')
- grad_lambda: float32 [24576], P('tile')
- grad_mu: float32 [24576], P('tile')
Inputs may be any that keep to these rules, and one draw needn't show every extreme that they name: `columns`: slot 0 of every block names the block itself (its index within the tile); in every tile, slot 3 of block 0 names pool block 12 and slot 3 of block 11 names pool block 27; the other slots name any block of the pool. Entries send_list[t, 1, 0] and send_list[t, 0, 7] are never 0. `counts`: some tile is full.
All inputs are finite; a program needn't handle non-finite values.
Results may differ from a plain program's by a relative error of at most 0.0001.
Values sent between devices are 32-bit elements; how exact they have to be, the bound alone decides.
No kernel may reach another device: no remote copies, remote signals or barrier semaphores. Data moves between devices by JAX's collectives and lax.ppermute only.
A program may use at most 64 MiB of HBM per device.

v0:
```python
import jax
import jax.numpy as jnp
from jax import lax
from jax.sharding import PartitionSpec as P

ITERS = 6
HIGH = lax.Precision.HIGHEST
KAPPA = 0.5


def extended(shard, sides, width):
    for axis, dim in sides:
        size, length = (lax.axis_size(axis), shard.shape[dim])
        up = [(i, (i + 1) % size) for i in range(size - 1)]
        down = [(j, i) for i, j in up]
        last = lax.slice_in_dim(shard, length - width, length, axis=dim)
        leading = lax.slice_in_dim(shard, 0, width, axis=dim)
        before = lax.ppermute(last, axis, up)
        after = lax.ppermute(leading, axis, down)
        shard = jnp.concatenate([before, shard, after], axis=dim)
    return shard


def shards(load, target, lame_lambda, lame_mu, volume, smooth, columns, send_list, counts):
    cases = load.shape[0]
    nblk = smooth.shape[0]
    ghosts = send_list.shape[2]
    width = smooth.shape[3]
    pool_n = nblk + 2 * ghosts
    field_shape = (cases, 3, nblk, width)
    alive = (
        (jnp.arange(nblk * width, dtype=jnp.int32) < counts[0])
        .astype(jnp.float32)
        .reshape(nblk, width)
    )
    weight = volume.reshape(nblk, width) * alive
    lam_weight = weight * lame_lambda.reshape(nblk, width)
    shear_weight = weight * lame_mu.reshape(nblk, width)
    column_hot = (columns[:, :, None] == jnp.arange(pool_n, dtype=jnp.int32)[None, None, :]).astype(
        jnp.float32
    )
    block_range = jnp.arange(nblk, dtype=jnp.int32)
    identity = jnp.eye(3, dtype=jnp.float32)
    neighbors = extended(send_list, (("tile", 0),), 1)
    below_ids = neighbors[0, 1]
    above_ids = neighbors[2, 0]
    below_hot = (below_ids[:, None] == block_range[None, :]).astype(jnp.float32)
    above_hot = (above_ids[:, None] == block_range[None, :]).astype(jnp.float32)

    def collect(field):
        padded = extended(field, (("tile", 2),), nblk)
        from_left = jnp.take(padded[:, :, :nblk], below_ids, axis=2)
        from_right = jnp.take(padded[:, :, 2 * nblk :], above_ids, axis=2)
        return jnp.concatenate([field, from_left, from_right], axis=2)

    def send_back(lower_part, upper_part):
        to_lower = jnp.einsum("cegj,gb->cebj", lower_part, below_hot, precision=HIGH)
        to_upper = jnp.einsum("cegj,gb->cebj", upper_part, above_hot, precision=HIGH)
        padded = extended(jnp.concatenate([to_lower, to_upper], axis=2), (("tile", 2),), nblk)
        return padded[:, :, :nblk] + padded[:, :, 3 * nblk :]

    def strains(field):
        pooled = collect(field * alive)
        gathered = jnp.einsum("ceqj,bkq->cebkj", pooled, column_hot, precision=HIGH)
        return jnp.einsum("bkdij,cebkj->cedbi", smooth, gathered, precision=HIGH)

    def operate(field):
        grads = strains(field)
        trace_u = grads[:, 0, 0] + grads[:, 1, 1] + grads[:, 2, 2]
        strain = 0.5 * (grads + jnp.swapaxes(grads, 1, 2))
        stress = (
            2.0 * shear_weight * strain
            + (lam_weight * trace_u)[:, None, None] * identity[None, :, :, None, None]
        )
        contrib = jnp.einsum("bkdij,cedbi->cebkj", smooth, stress, precision=HIGH)
        pooled = jnp.einsum("cebkj,bkq->ceqj", contrib, column_hot, precision=HIGH)
        own = pooled[:, :, :nblk]
        returned = send_back(pooled[:, :, nblk : nblk + ghosts], pooled[:, :, nblk + ghosts :])
        return alive * (own + returned) + KAPPA * field

    def curvature(first, second):
        return lax.psum(jnp.sum(first * second, axis=(1, 2, 3)), "tile")

    def squares(residual):
        return lax.psum(jnp.sum(residual * residual, axis=(1, 2, 3)), "tile")

    def widen(scalars):
        return scalars[:, None, None, None]

    def run_solver(rhs):
        solution = jnp.zeros_like(rhs)
        residual = rhs
        direction = rhs
        norm_now = squares(residual)
        for sweep in range(ITERS):
            image = operate(direction)
            step_len = norm_now / curvature(direction, image)
            solution = solution + widen(step_len) * direction
            residual = residual - widen(step_len) * image
            norm_next = squares(residual)
            direction = residual + widen(norm_next / norm_now) * direction
            norm_now = norm_next
        return solution

    forward = run_solver(alive * load.reshape(field_shape))
    adjoint = run_solver(alive * (forward - target.reshape(field_shape)))
    grads = strains(jnp.concatenate([forward, adjoint], axis=0))
    grads_u = grads[:cases]
    grads_a = grads[cases:]
    trace_u = grads_u[:, 0, 0] + grads_u[:, 1, 1] + grads_u[:, 2, 2]
    trace_a = grads_a[:, 0, 0] + grads_a[:, 1, 1] + grads_a[:, 2, 2]
    strain_u = 0.5 * (grads_u + jnp.swapaxes(grads_u, 1, 2))
    strain_a = 0.5 * (grads_a + jnp.swapaxes(grads_a, 1, 2))
    local_lambda = (-weight * jnp.sum(trace_u * trace_a, axis=0)).reshape(-1)
    local_mu = (-2.0 * weight * jnp.sum(strain_u * strain_a, axis=(0, 1, 2))).reshape(-1)
    grad_lambda, grad_mu = lax.psum((local_lambda, local_mu), "case")
    return (forward.reshape(load.shape), grad_lambda, grad_mu)


def solution(mesh):
    return jax.shard_map(
        shards,
        mesh=mesh,
        in_specs=(
            P("case", None, "tile"),
            P("case", None, "tile"),
            P("tile"),
            P("tile"),
            P("tile"),
            P("tile", None, None, None, None),
            P("tile", None),
            P("tile", None, None),
            P("tile"),
        ),
        out_specs=(P("case", None, "tile"), P("tile"), P("tile")),
        check_vma=False,
    )
```

profile of v0, /device:TPU:0, one launch (start us, length us, event | category | flops | bytes accessed | tf_op | source)
XLA Modules:
  0.0 1096.6 jit_solution(6777021464076940048)
XLA Ops:
  2.1 2.4 collective-permute-start
  5.8 5.1 collective-permute-start.1
  13.1 2.4 collective-permute-done.3
  18.0 11.6 %fusion.48 = f32[12,2,3,3,128,1]{4,2,5,3,1,0:T(4,128)S(1)} fusion(f32[12,4,2,3,128]{4,0,3,2,1:T(8,128)S(1)} %fusion.161, f32[12,4,3,128,128]{4,3,2,1,0:T(8,128)} %param.18), kind=kOutput, calls=%fused_computation.74 | convolution fusion | flops 169869312 | bytes 9695232 | tf_op jit(solution)/shard_map/bkdij,cebkj->cedbi/dot_general | solution.py:65
  29.8 4.8 fusion.22
  36.8 4.9 collective-permute-start.4
  42.7 34.1 %all-reduce.1 = (f32[2]{0:T(128)S(1)}, f32[2]{0:T(128)S(1)}) all-reduce(f32[2]{0:T(128)S(1)} %multiply_reduce_fusion.21, f32[2]{0:T(128)S(1)} %multiply_reduce_fusion.20), channel_id=1, replica_groups=mesh['tile'=16,'case'=2] {'tile'}, use_global_device_ids=true, to_apply=%region_1.0 | all-reduce | flops 4 | bytes 32 | tf_op jit(solution)/shard_map/psum | solution.py:85
  76.9 29.5 %psum.184 = f32[2]{0:T(128)S(1)} all-reduce(f32[2]{0:T(128)S(1)} %get-tuple-element.69), channel_id=1, replica_groups=mesh['tile'=16,'case'=2] {'tile'}, use_global_device_ids=true, to_apply=%region_5.7 | all-reduce | flops 2 | bytes 16 | tf_op jit(solution)/shard_map/psum | solution.py:85
  112.4 10.5 fusion.46
  123.1 7.3 fusion.20
  132.6 4.8 collective-permute-start.8
  138.4 31.5 %psum.185 = f32[2]{0:T(128)S(1)} all-reduce(f32[2]{0:T(128)S(1)} %get-tuple-element.65), channel_id=1, replica_groups=mesh['tile'=16,'case'=2] {'tile'}, use_global_device_ids=true, to_apply=%region_7.9 | all-reduce | flops 2 | bytes 16 | tf_op jit(solution)/shard_map/psum | solution.py:82
  170.1 29.5 %psum.186 = f32[2]{0:T(128)S(1)} all-reduce(f32[2]{0:T(128)S(1)} %get-tuple-element.63), channel_id=1, replica_groups=mesh['tile'=16,'case'=2] {'tile'}, use_global_device_ids=true, to_apply=%region_9.11 | all-reduce | flops 2 | bytes 16 | tf_op jit(solution)/shard_map/psum | solution.py:85
  205.5 10.5 fusion.44
  216.2 7.3 fusion.18
  225.7 4.8 collective-permute-start.12
  231.5 31.5 %psum.187 = f32[2]{0:T(128)S(1)} all-reduce(f32[2]{0:T(128)S(1)} %get-tuple-element.59), channel_id=1, replica_groups=mesh['tile'=16,'case'=2] {'tile'}, use_global_device_ids=true, to_apply=%region_11.13 | all-reduce | flops 2 | bytes 16 | tf_op jit(solution)/shard_map/psum | solution.py:82
  263.2 29.5 %psum.188 = f32[2]{0:T(128)S(1)} all-reduce(f32[2]{0:T(128)S(1)} %get-tuple-element.57), channel_id=1, replica_groups=mesh['tile'=16,'case'=2] {'tile'}, use_global_device_ids=true, to_apply=%region_13.15 | all-reduce | flops 2 | bytes 16 | tf_op jit(solution)/shard_map/psum | solution.py:85
  298.6 10.5 fusion.42
  309.4 7.3 fusion.16
  318.8 4.8 collective-permute-start.16
  324.7 31.5 %psum.189 = f32[2]{0:T(128)S(1)} all-reduce(f32[2]{0:T(128)S(1)} %get-tuple-element.53), channel_id=1, replica_groups=mesh['tile'=16,'case'=2] {'tile'}, use_global_device_ids=true, to_apply=%region_15.17 | all-reduce | flops 2 | bytes 16 | tf_op jit(solution)/shard_map/psum | solution.py:82
  356.3 29.5 %psum.190 = f32[2]{0:T(128)S(1)} all-reduce(f32[2]{0:T(128)S(1)} %get-tuple-element.51), channel_id=1, replica_groups=mesh['tile'=16,'case'=2] {'tile'}, use_global_device_ids=true, to_apply=%region_17.19 | all-reduce | flops 2 | bytes 16 | tf_op jit(solution)/shard_map/psum | solution.py:85
  391.8 10.5 fusion.40
  402.5 7.3 fusion.14
  412.0 4.8 collective-permute-start.20
  417.8 31.5 %psum.191 = f32[2]{0:T(128)S(1)} all-reduce(f32[2]{0:T(128)S(1)} %get-tuple-element.47), channel_id=1, replica_groups=mesh['tile'=16,'case'=2] {'tile'}, use_global_device_ids=true, to_apply=%region_19.21 | all-reduce | flops 2 | bytes 16 | tf_op jit(solution)/shard_map/psum | solution.py:82
  449.5 29.5 %psum.192 = f32[2]{0:T(128)S(1)} all-reduce(f32[2]{0:T(128)S(1)} %multiply_reduce_fusion.11), channel_id=1, replica_groups=mesh['tile'=16,'case'=2] {'tile'}, use_global_device_ids=true, to_apply=%region_21.23 | all-reduce | flops 2 | bytes 16 | tf_op jit(solution)/shard_map/psum | solution.py:85
  484.9 10.5 fusion.38
  495.7 7.3 fusion.12
  505.1 4.8 collective-permute-start.24
  511.0 31.5 %psum.193 = f32[2]{0:T(128)S(1)} all-reduce(f32[2]{0:T(128)S(1)} %fusion.238), channel_id=1, replica_groups=mesh['tile'=16,'case'=2] {'tile'}, use_global_device_ids=true, to_apply=%region_23.25 | all-reduce | flops 2 | bytes 16 | tf_op jit(solution)/shard_map/psum | solution.py:82
  543.9 3.2 collective-permute-start.26
  548.8 10.5 fusion.36
  559.6 7.3 fusion.10
  569.0 3.0 collective-permute-start.28
  573.1 31.9 %all-reduce = (f32[2]{0:T(128)S(1)}, f32[2]{0:T(128)S(1)}) all-reduce(f32[2]{0:T(128)S(1)} %get-tuple-element.9, f32[2]{0:T(128)S(1)} %get-tuple-element.8), channel_id=1, replica_groups=mesh['tile'=16,'case'=2] {'tile'}, use_global_device_ids=true, to_apply=%region_25.27 | all-reduce | flops 4 | bytes 32 | tf_op jit(solution)/shard_map/psum | solution.py:85
  605.2 29.5 %psum.196 = f32[2]{0:T(128)S(1)} all-reduce(f32[2]{0:T(128)S(1)} %get-tuple-element.40), channel_id=1, replica_groups=mesh['tile'=16,'case'=2] {'tile'}, use_global_device_ids=true, to_apply=%region_29.31 | all-reduce | flops 2 | bytes 16 | tf_op jit(solution)/shard_map/psum | solution.py:85
  640.6 10.5 fusion.34
  651.3 7.3 fusion.8
  660.8 4.8 collective-permute-start.32
  666.6 31.5 %psum.197 = f32[2]{0:T(128)S(1)} all-reduce(f32[2]{0:T(128)S(1)} %get-tuple-element.36), channel_id=1, replica_groups=mesh['tile'=16,'case'=2] {'tile'}, use_global_device_ids=true, to_apply=%region_31.33 | all-reduce | flops 2 | bytes 16 | tf_op jit(solution)/shard_map/psum | solution.py:82
  698.3 29.5 %psum.198 = f32[2]{0:T(128)S(1)} all-reduce(f32[2]{0:T(128)S(1)} %get-tuple-element.34), channel_id=1, replica_groups=mesh['tile'=16,'case'=2] {'tile'}, use_global_device_ids=true, to_apply=%region_33.35 | all-reduce | flops 2 | bytes 16 | tf_op jit(solution)/shard_map/psum | solution.py:85
  733.7 10.5 fusion.32
  744.5 7.3 fusion.6
  753.9 4.8 collective-permute-start.36
  759.7 31.5 %psum.199 = f32[2]{0:T(128)S(1)} all-reduce(f32[2]{0:T(128)S(1)} %get-tuple-element.30), channel_id=1, replica_groups=mesh['tile'=16,'case'=2] {'tile'}, use_global_device_ids=true, to_apply=%region_35.37 | all-reduce | flops 2 | bytes 16 | tf_op jit(solution)/shard_map/psum | solution.py:82
  791.4 29.5 %psum.200 = f32[2]{0:T(128)S(1)} all-reduce(f32[2]{0:T(128)S(1)} %get-tuple-element.28), channel_id=1, replica_groups=mesh['tile'=16,'case'=2] {'tile'}, use_global_device_ids=true, to_apply=%region_37.39 | all-reduce | flops 2 | bytes 16 | tf_op jit(solution)/shard_map/psum | solution.py:85
  826.9 10.5 fusion.30
  837.6 7.3 fusion.4
  847.1 4.8 collective-permute-start.40
  852.9 31.5 %psum.201 = f32[2]{0:T(128)S(1)} all-reduce(f32[2]{0:T(128)S(1)} %get-tuple-element.24), channel_id=1, replica_groups=mesh['tile'=16,'case'=2] {'tile'}, use_global_device_ids=true, to_apply=%region_39.41 | all-reduce | flops 2 | bytes 16 | tf_op jit(solution)/shard_map/psum | solution.py:82
  884.6 29.5 %psum.202 = f32[2]{0:T(128)S(1)} all-reduce(f32[2]{0:T(128)S(1)} %get-tuple-element.22), channel_id=1, replica_groups=mesh['tile'=16,'case'=2] {'tile'}, use_global_device_ids=true, to_apply=%region_41.43 | all-reduce | flops 2 | bytes 16 | tf_op jit(solution)/shard_map/psum | solution.py:85
  920.0 10.5 fusion.28
  930.7 7.3 fusion.2
  940.2 4.8 collective-permute-start.44
  946.0 31.5 %psum.203 = f32[2]{0:T(128)S(1)} all-reduce(f32[2]{0:T(128)S(1)} %get-tuple-element.18), channel_id=1, replica_groups=mesh['tile'=16,'case'=2] {'tile'}, use_global_device_ids=true, to_apply=%region_43.45 | all-reduce | flops 2 | bytes 16 | tf_op jit(solution)/shard_map/psum | solution.py:82
  977.7 29.5 %psum.204 = f32[2]{0:T(128)S(1)} all-reduce(f32[2]{0:T(128)S(1)} %multiply_reduce_fusion), channel_id=1, replica_groups=mesh['tile'=16,'case'=2] {'tile'}, use_global_device_ids=true, to_apply=%region_45.47 | all-reduce | flops 2 | bytes 16 | tf_op jit(solution)/shard_map/psum | solution.py:85
  1013.2 10.5 fusion.26
  1023.9 7.3 fusion
  1033.4 4.8 collective-permute-start.48
  1039.2 31.5 %psum.205 = f32[2]{0:T(128)S(1)} all-reduce(f32[2]{0:T(128)S(1)} %fusion.224), channel_id=1, replica_groups=mesh['tile'=16,'case'=2] {'tile'}, use_global_device_ids=true, to_apply=%region_47.49 | all-reduce | flops 2 | bytes 16 | tf_op jit(solution)/shard_map/psum | solution.py:82
  1077.0 10.5 fusion.50
  1087.8 8.7 all-reduce.2
  (337 shorter events, 116.8 us)
Async XLA Ops:
  2.1 13.4 %collective-permute-start = (f32[2,3,12,128]{3,2,1,0:T(8,128)S(1)}, f32[2,3,12,128]{3,2,1,0:T(8,128)S(1)}, u32[]{:S(2)}, u32[]{:S(2)}) collective-permute-start(f32[2,3,12,128]{3,2,1,0:T(8,128)S(1)} %broadcast_multiply_fusion.11), channel_id=1, source_target_pairs={{0,2},{2,4},{4,6},{6,8},{8,10},{10,12},{12,14},{14,16},{16,18},{18... | collective-permute-start | bytes 110600 | tf_op jit(solution)/shard_map/ppermute | solution.py:18
  4.5 11.6 %collective-permute-start.2 = (f32[2,3,12,128]{3,2,1,0:T(8,128)S(1)}, f32[2,3,12,128]{3,2,1,0:T(8,128)S(1)}, u32[]{:S(2)}, u32[]{:S(2)}) collective-permute-start(f32[2,3,12,128]{3,2,1,0:T(8,128)S(1)} %broadcast_multiply_fusion.11), channel_id=1, source_target_pairs={{2,0},{4,2},{6,4},{8,6},{10,8},{12,10},{14,12},{16,14},{18,16},{20... | collective-permute-start | bytes 110600 | tf_op jit(solution)/shard_map/ppermute | solution.py:19
  5.8 7.2 collective-permute-start.1
  11.0 4.5 collective-permute-start.3
  16.7 13.0 %copy-start = (f32[12,4,3,128,128]{4,3,2,1,0:T(8,128)S(1)}, f32[12,4,3,128,128]{4,3,2,1,0:T(8,128)}, u32[]{:S(2)}) copy-start(f32[12,4,3,128,128]{4,3,2,1,0:T(8,128)} %param.18) | copy-start | bytes 28311556
  17.9 16.7 %copy-start.1 = (s32[12,4]{0,1:T(4,128)S(1)}, s32[12,4]{0,1:T(4,128)}, u32[]{:S(2)}) copy-start(s32[12,4]{0,1:T(4,128)} %param.19) | copy-start | bytes 580
  18.0 23.7 %copy-start.2 = (f32[2,3,1536]{2,0,1:T(2,128)S(1)}, f32[2,3,1536]{2,0,1:T(2,128)}, u32[]{:S(2)}) copy-start(f32[2,3,1536]{2,0,1:T(2,128)} %param.13) | copy-start | bytes 110596
  35.2 6.6 collective-permute-start.5
  36.8 5.7 collective-permute-start.4
  106.5 3.2 collective-permute-start.6
  108.3 3.1 collective-permute-start.7
  131.3 6.1 collective-permute-start.9
  132.6 5.7 collective-permute-start.8
  199.6 3.3 collective-permute-start.10
  201.4 3.1 collective-permute-start.11
  224.4 6.1 collective-permute-start.13
  225.7 5.7 collective-permute-start.12
  292.8 3.3 collective-permute-start.14
  294.5 3.1 collective-permute-start.15
  317.5 6.1 collective-permute-start.17
  318.8 5.7 collective-permute-start.16
  385.9 3.4 collective-permute-start.18
  387.7 3.1 collective-permute-start.19
  410.7 6.1 collective-permute-start.21
  412.0 5.7 collective-permute-start.20
  479.1 3.6 collective-permute-start.22
  480.8 3.1 collective-permute-start.23
  484.9 26.0 %copy-start.3 = (f32[2,3,1536]{2,0,1:T(2,128)S(1)}, f32[2,3,1536]{2,0,1:T(2,128)}, u32[]{:S(2)}) copy-start(f32[2,3,1536]{2,0,1:T(2,128)} %param.14) | copy-start | bytes 110596
  503.8 6.1 collective-permute-start.25
  505.1 5.7 collective-permute-start.24
  542.6 4.5 collective-permute-start.27
  543.9 3.9 collective-permute-start.26
  567.7 4.3 collective-permute-start.29
  569.0 3.9 collective-permute-start.28
  634.7 3.3 collective-permute-start.30
  636.5 3.1 collective-permute-start.31
  659.5 6.1 collective-permute-start.33
  660.8 5.7 collective-permute-start.32
  727.9 3.3 collective-permute-start.34
  729.6 3.1 collective-permute-start.35
  752.6 6.1 collective-permute-start.37
  753.9 5.7 collective-permute-start.36
  821.0 3.4 collective-permute-start.38
  822.8 3.1 collective-permute-start.39
  845.8 6.1 collective-permute-start.41
  847.1 5.7 collective-permute-start.40
  914.1 3.6 collective-permute-start.42
  915.9 3.1 collective-permute-start.43
  938.9 6.1 collective-permute-start.45
  940.2 5.7 collective-permute-start.44
  1007.3 3.3 collective-permute-start.46
  1009.1 3.1 collective-permute-start.47
  1023.9 63.8 %copy-start.4 = (f32[1536]{0:T(1024)S(1)}, f32[1536]{0:T(1024)}, u32[]{:S(2)}) copy-start(f32[1536]{0:T(1024)} %param.17) | copy-start | bytes 18436
  1032.1 6.1 collective-permute-start.49
  1033.4 5.7 collective-permute-start.48
  1070.8 3.3 collective-permute-start.50
  1072.8 3.2 collective-permute-start.51
where the time goes:
time: 1110 us; the launch traced here: 1100 us
  blocking collectives  684 us (62%)
  matrix products  238 us (21%)
  starting transfers between devices  122 us (11%)
  waiting for transfers between devices  22 us (2%)
  local copies, waits for them, and re-layouts  17.9 us (2%)
    psum x12, blocking collectives, squares(): return lax.psum(jnp.sum(residual * residual, axis=(1, 2, 3)), 'tile')  361 us
    psum x10, blocking collectives, curvature(): return lax.psum(jnp.sum(first * second, axis=(1, 2, 3)), 'tile')  315 us
    dot_general x13, matrix products, strains(): return jnp.einsum('bkdij,cebkj->cedbi', smooth, gathered, precision=HIGH)  138 us
    ppermute x26, starting transfers between devices, extended(): before = lax.ppermute(last, axis, up)  85.9 us
    dot_general x12, matrix products, operate(): contrib = jnp.einsum('bkdij,cedbi->cebkj', smooth, stress, precision=HIGH)  84.8 us
    ppermute x26, starting transfers between devices, extended(): after = lax.ppermute(leading, axis, down)  36.5 us
  transfers between devices with their start and end apart: 52, of which 24 were waited for; matrix products, arithmetic and copies ran while one was open for 1% of the time, Pallas kernels for 0%

commit v1 on v0

--- a/solution.py
+++ b/solution.py
@@ -6,6 +6,11 @@
 ITERS = 6
 HIGH = lax.Precision.HIGHEST
 KAPPA = 0.5
+
+
+def add_all(x, axis):
+    parts = lax.all_gather(x, axis)
+    return jnp.sum(parts, axis=0)
 
 
 def extended(shard, sides, width):
@@ -82,7 +87,7 @@
         return lax.psum(jnp.sum(first * second, axis=(1, 2, 3)), "tile")
 
     def squares(residual):
-        return lax.psum(jnp.sum(residual * residual, axis=(1, 2, 3)), "tile")
+        return add_all(jnp.sum(residual * residual, axis=(1, 2, 3)), "tile")
 
     def widen(scalars):
         return scalars[:, None, None, None]

time: 1110 us -> 1110 us (level)
    psum x12 -> x0, blocking collectives: 361 us -> none  [squares(): return lax.psum(jnp.sum(residual * residual, axis=(1, 2, 3)), 'tile')]
    unnamed x0 -> x12, blocking collectives: none -> 360 us
  transfers between devices with their start and end apart: 52 -> 52, of which waited for: 24 -> 23; matrix products, arithmetic and copies ran while one was open for 1% -> 1% of each run, Pallas kernels for 0% -> 0%
where the time goes in v1:
time: 1110 us; the launch traced here: 1100 us
  blocking collectives  683 us (62%)
  matrix products  238 us (21%)
  starting transfers between devices  122 us (11%)
  local copies, waits for them, and re-layouts  22 us (2%)
  waiting for transfers between devices  21.5 us (2%)
    unnamed x12, blocking collectives  360 us
    psum x10, blocking collectives, curvature(): return lax.psum(jnp.sum(first * second, axis=(1, 2, 3)), 'tile')  315 us
    dot_general x13, matrix products, strains(): return jnp.einsum('bkdij,cebkj->cedbi', smooth, gathered, precision=HIGH)  138 us
    ppermute x26, starting transfers between devices, extended(): before = lax.ppermute(last, axis, up)  86 us
    dot_general x12, matrix products, operate(): contrib = jnp.einsum('bkdij,cedbi->cebkj', smooth, stress, precision=HIGH)  84.8 us
    ppermute x26, starting transfers between devices, extended(): after = lax.ppermute(leading, axis, down)  36.3 us
  transfers between devices with their start and end apart: 52, of which 23 were waited for; matrix products, arithmetic and copies ran while one was open for 1% of the time, Pallas kernels for 0%

profile of v1, /device:TPU:0, one launch (start us, length us, event | category | flops | bytes accessed | tf_op | source)
XLA Modules:
  0.0 1100.6 jit_solution(5524224031820667939)
XLA Ops:
  2.1 2.4 collective-permute-start
  5.8 5.1 collective-permute-start.1
  13.1 2.4 collective-permute-done.3
  18.0 11.6 %fusion.48 = f32[12,2,3,3,128,1]{4,2,5,3,1,0:T(4,128)S(1)} fusion(f32[12,4,2,3,128]{4,0,3,2,1:T(8,128)S(1)} %fusion.161, f32[12,4,3,128,128]{4,3,2,1,0:T(8,128)} %param.18), kind=kOutput, calls=%fused_computation.74 | convolution fusion | flops 169869312 | bytes 9695232 | tf_op jit(solution)/shard_map/bkdij,cebkj->cedbi/dot_general | solution.py:70
  29.8 4.8 fusion.22
  36.8 4.9 collective-permute-start.4
  43.5 33.3 %all-reduce.13 = (f32[32]{0:T(128)S(1)}, f32[2]{0:T(128)S(1)}) all-reduce(f32[32]{0:T(128)S(1)} %dynamic-update-slice, f32[2]{0:T(128)S(1)} %multiply_reduce_fusion.20), channel_id=2, replica_groups=mesh['tile'=16,'case'=2] {'tile'}, use_global_device_ids=true, to_apply=%add | all-reduce | flops 34 | bytes 272
  77.3 29.5 %all-reduce.1 = f32[32]{0:T(128)S(1)} all-reduce(f32[32]{0:T(128)S(1)} %dynamic-update-slice.1), channel_id=3, replica_groups=mesh['tile'=16,'case'=2] {'tile'}, use_global_device_ids=true, to_apply=%add.1 | all-reduce | flops 32 | bytes 256
  112.8 10.5 fusion.46
  123.5 7.3 fusion.20
  133.0 4.8 collective-permute-start.8
  138.8 31.5 %psum.99 = f32[2]{0:T(128)S(1)} all-reduce(f32[2]{0:T(128)S(1)} %get-tuple-element.65), channel_id=1, replica_groups=mesh['tile'=16,'case'=2] {'tile'}, use_global_device_ids=true, to_apply=%region_7.9 | all-reduce | flops 2 | bytes 16 | tf_op jit(solution)/shard_map/psum | solution.py:87
  170.7 29.5 %all-reduce.2 = f32[32]{0:T(128)S(1)} all-reduce(f32[32]{0:T(128)S(1)} %dynamic-update-slice.2), channel_id=4, replica_groups=mesh['tile'=16,'case'=2] {'tile'}, use_global_device_ids=true, to_apply=%add.2 | all-reduce | flops 32 | bytes 256
  206.3 10.5 fusion.44
  217.0 7.3 fusion.18
  226.5 4.8 collective-permute-start.12
  232.3 31.5 %psum.100 = f32[2]{0:T(128)S(1)} all-reduce(f32[2]{0:T(128)S(1)} %get-tuple-element.59), channel_id=1, replica_groups=mesh['tile'=16,'case'=2] {'tile'}, use_global_device_ids=true, to_apply=%region_11.13 | all-reduce | flops 2 | bytes 16 | tf_op jit(solution)/shard_map/psum | solution.py:87
  264.2 29.5 %all-reduce.3 = f32[32]{0:T(128)S(1)} all-reduce(f32[32]{0:T(128)S(1)} %dynamic-update-slice.3), channel_id=5, replica_groups=mesh['tile'=16,'case'=2] {'tile'}, use_global_device_ids=true, to_apply=%add.3 | all-reduce | flops 32 | bytes 256
  299.7 10.5 fusion.42
  310.5 7.3 fusion.16
  319.9 4.8 collective-permute-start.16
  325.8 31.5 %psum.101 = f32[2]{0:T(128)S(1)} all-reduce(f32[2]{0:T(128)S(1)} %get-tuple-element.53), channel_id=1, replica_groups=mesh['tile'=16,'case'=2] {'tile'}, use_global_device_ids=true, to_apply=%region_15.17 | all-reduce | flops 2 | bytes 16 | tf_op jit(solution)/shard_map/psum | solution.py:87
  357.6 29.5 %all-reduce.4 = f32[32]{0:T(128)S(1)} all-reduce(f32[32]{0:T(128)S(1)} %dynamic-update-slice.4), channel_id=6, replica_groups=mesh['tile'=16,'case'=2] {'tile'}, use_global_device_ids=true, to_apply=%add.4 | all-reduce | flops 32 | bytes 256
  393.2 10.5 fusion.40
  403.9 7.3 fusion.14
  413.4 4.8 collective-permute-start.20
  419.2 31.5 %psum.102 = f32[2]{0:T(128)S(1)} all-reduce(f32[2]{0:T(128)S(1)} %get-tuple-element.47), channel_id=1, replica_groups=mesh['tile'=16,'case'=2] {'tile'}, use_global_device_ids=true, to_apply=%region_19.21 | all-reduce | flops 2 | bytes 16 | tf_op jit(solution)/shard_map/psum | solution.py:87
  451.1 29.5 %all-reduce.5 = f32[32]{0:T(128)S(1)} all-reduce(f32[32]{0:T(128)S(1)} %dynamic-update-slice.5), channel_id=7, replica_groups=mesh['tile'=16,'case'=2] {'tile'}, use_global_device_ids=true, to_apply=%add.5 | all-reduce | flops 32 | bytes 256
  486.7 10.5 fusion.38
  497.4 7.3 fusion.12
  506.9 4.8 collective-permute-start.24
  512.7 31.5 %psum.103 = f32[2]{0:T(128)S(1)} all-reduce(f32[2]{0:T(128)S(1)} %fusion.238), channel_id=1, replica_groups=mesh['tile'=16,'case'=2] {'tile'}, use_global_device_ids=true, to_apply=%region_23.25 | all-reduce | flops 2 | bytes 16 | tf_op jit(solution)/shard_map/psum | solution.py:87
  545.7 3.3 collective-permute-start.26
  550.6 10.5 fusion.36
  561.4 7.3 fusion.10
  570.8 3.0 collective-permute-start.28
  575.1 31.8 %all-reduce.12 = (f32[32]{0:T(128)S(1)}, f32[2]{0:T(128)S(1)}) all-reduce(f32[32]{0:T(128)S(1)} %dynamic-update-slice.6, f32[2]{0:T(128)S(1)} %get-tuple-element.8), channel_id=8, replica_groups=mesh['tile'=16,'case'=2] {'tile'}, use_global_device_ids=true, to_apply=%add.6 | all-reduce | flops 34 | bytes 272
  607.4 29.5 %all-reduce.7 = f32[32]{0:T(128)S(1)} all-reduce(f32[32]{0:T(128)S(1)} %dynamic-update-slice.7), channel_id=9, replica_groups=mesh['tile'=16,'case'=2] {'tile'}, use_global_device_ids=true, to_apply=%add.7 | all-reduce | flops 32 | bytes 256
  643.0 10.5 fusion.34
  653.7 7.3 fusion.8
  663.2 4.8 collective-permute-start.32
  669.0 31.5 %psum.105 = f32[2]{0:T(128)S(1)} all-reduce(f32[2]{0:T(128)S(1)} %get-tuple-element.36), channel_id=1, replica_groups=mesh['tile'=16,'case'=2] {'tile'}, use_global_device_ids=true, to_apply=%region_31.33 | all-reduce | flops 2 | bytes 16 | tf_op jit(solution)/shard_map/psum | solution.py:87
  700.9 29.5 %all-reduce.8 = f32[32]{0:T(128)S(1)} all-reduce(f32[32]{0:T(128)S(1)} %dynamic-update-slice.8), channel_id=10, replica_groups=mesh['tile'=16,'case'=2] {'tile'}, use_global_device_ids=true, to_apply=%add.8 | all-reduce | flops 32 | bytes 256
  736.4 10.5 fusion.32
  747.2 7.3 fusion.6
  756.6 4.8 collective-permute-start.36
  762.5 31.5 %psum.106 = f32[2]{0:T(128)S(1)} all-reduce(f32[2]{0:T(128)S(1)} %get-tuple-element.30), channel_id=1, replica_groups=mesh['tile'=16,'case'=2] {'tile'}, use_global_device_ids=true, to_apply=%region_35.37 | all-reduce | flops 2 | bytes 16 | tf_op jit(solution)/shard_map/psum | solution.py:87
  794.3 29.5 %all-reduce.9 = f32[32]{0:T(128)S(1)} all-reduce(f32[32]{0:T(128)S(1)} %dynamic-update-slice.9), channel_id=11, replica_groups=mesh['tile'=16,'case'=2] {'tile'}, use_global_device_ids=true, to_apply=%add.9 | all-reduce | flops 32 | bytes 256
  829.9 10.5 fusion.30
  840.6 7.3 fusion.4
  850.1 4.8 collective-permute-start.40
  855.9 31.5 %psum.107 = f32[2]{0:T(128)S(1)} all-reduce(f32[2]{0:T(128)S(1)} %get-tuple-element.24), channel_id=1, replica_groups=mesh['tile'=16,'case'=2] {'tile'}, use_global_device_ids=true, to_apply=%region_39.41 | all-reduce | flops 2 | bytes 16 | tf_op jit(solution)/shard_map/psum | solution.py:87
  887.8 29.5 %all-reduce.10 = f32[32]{0:T(128)S(1)} all-reduce(f32[32]{0:T(128)S(1)} %dynamic-update-slice.10), channel_id=12, replica_groups=mesh['tile'=16,'case'=2] {'tile'}, use_global_device_ids=true, to_apply=%add.10 | all-reduce | flops 32 | bytes 256
  923.4 10.5 fusion.28
  934.1 7.3 fusion.2
  943.6 4.8 collective-permute-start.44
  949.4 31.5 %psum.108 = f32[2]{0:T(128)S(1)} all-reduce(f32[2]{0:T(128)S(1)} %get-tuple-element.18), channel_id=1, replica_groups=mesh['tile'=16,'case'=2] {'tile'}, use_global_device_ids=true, to_apply=%region_43.45 | all-reduce | flops 2 | bytes 16 | tf_op jit(solution)/shard_map/psum | solution.py:87
  981.3 29.5 %all-reduce.11 = f32[32]{0:T(128)S(1)} all-reduce(f32[32]{0:T(128)S(1)} %dynamic-update-slice.11), channel_id=13, replica_groups=mesh['tile'=16,'case'=2] {'tile'}, use_global_device_ids=true, to_apply=%add.11 | all-reduce | flops 32 | bytes 256
  1016.8 10.5 fusion.26
  1027.6 7.3 fusion
  1037.0 4.8 collective-permute-start.48
  1042.9 31.5 %psum.109 = f32[2]{0:T(128)S(1)} all-reduce(f32[2]{0:T(128)S(1)} %fusion.224), channel_id=1, replica_groups=mesh['tile'=16,'case'=2] {'tile'}, use_global_device_ids=true, to_apply=%region_47.49 | all-reduce | flops 2 | bytes 16 | tf_op jit(solution)/shard_map/psum | solution.py:87
  1080.7 10.5 fusion.50
  1091.4 8.7 all-reduce.14
  (388 shorter events, 120.5 us)
Async XLA Ops:
  2.1 13.4 %collective-permute-start = (f32[2,3,12,128]{3,2,1,0:T(8,128)S(1)}, f32[2,3,12,128]{3,2,1,0:T(8,128)S(1)}, u32[]{:S(2)}, u32[]{:S(2)}) collective-permute-start(f32[2,3,12,128]{3,2,1,0:T(8,128)S(1)} %broadcast_multiply_fusion.11), channel_id=1, source_target_pairs={{0,2},{2,4},{4,6},{6,8},{8,10},{10,12},{12,14},{14,16},{16,18},{18... | collective-permute-start | bytes 110600 | tf_op jit(solution)/shard_map/ppermute | solution.py:23
  4.5 11.6 %collective-permute-start.2 = (f32[2,3,12,128]{3,2,1,0:T(8,128)S(1)}, f32[2,3,12,128]{3,2,1,0:T(8,128)S(1)}, u32[]{:S(2)}, u32[]{:S(2)}) collective-permute-start(f32[2,3,12,128]{3,2,1,0:T(8,128)S(1)} %broadcast_multiply_fusion.11), channel_id=1, source_target_pairs={{2,0},{4,2},{6,4},{8,6},{10,8},{12,10},{14,12},{16,14},{18,16},{20... | collective-permute-start | bytes 110600 | tf_op jit(solution)/shard_map/ppermute | solution.py:24
  5.8 7.2 collective-permute-start.1
  11.0 4.5 collective-permute-start.3
  16.7 13.0 %copy-start = (f32[12,4,3,128,128]{4,3,2,1,0:T(8,128)S(1)}, f32[12,4,3,128,128]{4,3,2,1,0:T(8,128)}, u32[]{:S(2)}) copy-start(f32[12,4,3,128,128]{4,3,2,1,0:T(8,128)} %param.18) | copy-start | bytes 28311556
  17.9 16.7 %copy-start.1 = (s32[12,4]{0,1:T(4,128)S(1)}, s32[12,4]{0,1:T(4,128)}, u32[]{:S(2)}) copy-start(s32[12,4]{0,1:T(4,128)} %param.19) | copy-start | bytes 580
  18.0 23.7 %copy-start.2 = (f32[2,3,1536]{2,0,1:T(2,128)S(1)}, f32[2,3,1536]{2,0,1:T(2,128)}, u32[]{:S(2)}) copy-start(f32[2,3,1536]{2,0,1:T(2,128)} %param.13) | copy-start | bytes 110596
  18.0 23.9 %copy-start.5 = (u32[32]{0:T(128)S(1)}, u32[32]{0:T(128)}, u32[]{:S(2)}) copy-start(u32[32]{0:T(128)} %constant.43) | copy-start | bytes 388
  35.2 8.1 collective-permute-start.5
  36.8 6.5 collective-permute-start.4
  106.9 3.3 collective-permute-start.6
  108.7 3.1 collective-permute-start.7
  131.7 6.1 collective-permute-start.9
  133.0 5.7 collective-permute-start.8
  200.4 3.3 collective-permute-start.10
  202.2 3.1 collective-permute-start.11
  225.2 6.1 collective-permute-start.13
  226.5 5.7 collective-permute-start.12
  293.9 3.5 collective-permute-start.14
  295.6 3.1 collective-permute-start.15
  318.6 6.1 collective-permute-start.17
  319.9 5.7 collective-permute-start.16
  387.3 3.3 collective-permute-start.18
  389.1 3.1 collective-permute-start.19
  412.1 6.1 collective-permute-start.21
  413.4 5.7 collective-permute-start.20
  480.8 3.3 collective-permute-start.22
  482.6 3.1 collective-permute-start.23
  486.7 26.0 %copy-start.3 = (f32[2,3,1536]{2,0,1:T(2,128)S(1)}, f32[2,3,1536]{2,0,1:T(2,128)}, u32[]{:S(2)}) copy-start(f32[2,3,1536]{2,0,1:T(2,128)} %param.14) | copy-start | bytes 110596
  505.6 6.1 collective-permute-start.25
  506.9 5.7 collective-permute-start.24
  544.4 4.6 collective-permute-start.27
  545.7 4.0 collective-permute-start.26
  569.5 4.3 collective-permute-start.29
  570.8 3.9 collective-permute-start.28
  637.1 3.5 collective-permute-start.30
  638.9 3.1 collective-permute-start.31
  661.9 6.1 collective-permute-start.33
  663.2 5.7 collective-permute-start.32
  730.6 3.3 collective-permute-start.34
  732.3 3.1 collective-permute-start.35
  755.3 6.1 collective-permute-start.37
  756.6 5.7 collective-permute-start.36
  824.0 3.3 collective-permute-start.38
  825.8 3.1 collective-permute-start.39
  848.8 6.1 collective-permute-start.41
  850.1 5.7 collective-permute-start.40
  917.5 3.3 collective-permute-start.42
  919.3 3.1 collective-permute-start.43
  942.3 6.1 collective-permute-start.45
  943.6 5.7 collective-permute-start.44
  1010.9 3.4 collective-permute-start.46
  1012.7 3.1 collective-permute-start.47
  1027.6 63.8 %copy-start.4 = (f32[1536]{0:T(1024)S(1)}, f32[1536]{0:T(1024)}, u32[]{:S(2)}) copy-start(f32[1536]{0:T(1024)} %param.17) | copy-start | bytes 18436
  1035.7 6.1 collective-permute-start.49
  1037.0 5.7 collective-permute-start.48
  1074.5 3.3 collective-permute-start.50
  1076.4 3.2 collective-permute-start.51
